TPU v7x, 128 devices: a whole 4x4x4 slice. The times are simulated.
128 devices in a mesh: expert: 8 (over x, core), cuts: 16 (over y, z).
Axes of the slice: x: 4, y: 4, z: 4, core: 2. Of those that a mesh axis runs over, the one named last changes fastest.
Arguments:
- tokens: bfloat16 [1024, 4096], P('expert', 'cuts'), may hold values from -6 to 6
- routing: int32 [1024, 2], P('expert'), may hold values from 0 to 7, all different within a row; in each aligned block of 128 rows (0 to 127, 128 to 255, ...) at most 64 rows name the same one
- gates: float32 [1024, 2], P('expert'), may hold values from 0.2 to 1
- cotangent: bfloat16 [1024, 4096], P('expert', 'cuts'), may hold values from -6 to 6
- w_gate: bfloat16 [8, 4096, 8192], P('expert', None, 'cuts'), may hold values from -0.09375 to 0.09375
- w_up: bfloat16 [8, 4096, 8192], P('expert', None, 'cuts'), may hold values from -0.09375 to 0.09375
- w_down: bfloat16 [8, 8192, 4096], P('expert', 'cuts'), may hold values from -0.0625 to 0.0625
Outputs:
- mixed: bfloat16 [1024, 4096], P('expert', 'cuts')
- grad_tokens: bfloat16 [1024, 4096], P('expert', 'cuts')
- grad_gates: float32 [1024, 2], P('expert')
- grad_w_gate: bfloat16 [8, 4096, 8192], P('expert', None, 'cuts')
- grad_w_up: bfloat16 [8, 4096, 8192], P('expert', None, 'cuts')
- grad_w_down: bfloat16 [8, 8192, 4096], P('expert', 'cuts')
Inputs may be any that keep to these rules, and one draw needn't show every extreme that they name: `routing`: in each aligned block of 128 rows (the tokens owned by one position along `expert`) no expert is named by more than 64 rows, a bound that some block reaches.
All inputs are finite; a program needn't handle non-finite values.
Results may differ from a plain program's by a relative error of at most 0.015.
Values may be sent and summed in bfloat16 or wider, within the bound.
A program may use at most 128 MiB of HBM per device.

v0:
```python
import jax
import jax.numpy as jnp
from jax import lax
from jax.sharding import PartitionSpec as P


def slot_tables(routing, experts, capacity):
    row_count = routing.shape[0]
    flat_route = routing.reshape(-1)
    onehot = (flat_route[:, None] == jnp.arange(experts, dtype=jnp.int32)[None, :]).astype(
        jnp.int32
    )
    before = jnp.cumsum(onehot, axis=0) - onehot
    position = jnp.sum(before * onehot, axis=1)
    destination = (flat_route * capacity + position).reshape(row_count, 2)
    slot_ids = jnp.arange(experts * capacity, dtype=jnp.int32)
    pick_first = (slot_ids[:, None] == destination[None, :, 0]).astype(jnp.bfloat16)
    pick_second = (slot_ids[:, None] == destination[None, :, 1]).astype(jnp.bfloat16)
    return (destination, pick_first, pick_second)


def local(tokens, routing, gates, cotangent, w_gate, w_up, w_down):
    experts = lax.axis_size("expert")
    capacity = tokens.shape[0] // 2
    destination, pick_first, pick_second = slot_tables(routing, experts, capacity)
    x_send = jnp.dot(pick_first + pick_second, tokens, preferred_element_type=jnp.float32).astype(
        jnp.bfloat16
    )
    grad_out = cotangent.astype(jnp.float32)
    grad_first = (gates[:, 0:1] * grad_out).astype(jnp.bfloat16)
    grad_second = (gates[:, 1:2] * grad_out).astype(jnp.bfloat16)
    d_send = (
        jnp.dot(pick_first, grad_first, preferred_element_type=jnp.float32)
        + jnp.dot(pick_second, grad_second, preferred_element_type=jnp.float32)
    ).astype(jnp.bfloat16)
    x_recv, d_recv = (
        lax.all_to_all(x_send, "expert", split_axis=0, concat_axis=0, tiled=True),
        lax.all_to_all(d_send, "expert", split_axis=0, concat_axis=0, tiled=True),
    )
    x_rows, d_rows = (
        lax.all_gather(x_recv, "cuts", axis=1, tiled=True),
        lax.all_gather(d_recv, "cuts", axis=1, tiled=True),
    )

    def send_home(partial_value):
        owned_sum = lax.psum_scatter(
            partial_value.astype(jnp.bfloat16), "cuts", scatter_dimension=1, tiled=True
        )
        return lax.all_to_all(owned_sum, "expert", split_axis=0, concat_axis=0, tiled=True)

    gate_w = w_gate[0]
    up_w = w_up[0]
    down_w = w_down[0]
    gate_pre = jnp.dot(x_rows, gate_w, preferred_element_type=jnp.float32)
    up_pre = jnp.dot(x_rows, up_w, preferred_element_type=jnp.float32)
    sigmoid_gate = jax.nn.sigmoid(gate_pre)
    activated = gate_pre * sigmoid_gate
    hidden = (activated * up_pre).astype(jnp.bfloat16)
    out_partial = jnp.dot(hidden, down_w, preferred_element_type=jnp.float32)
    out_home = send_home(out_partial)
    out_first = out_home[destination[:, 0]].astype(jnp.float32)
    out_second = out_home[destination[:, 1]].astype(jnp.float32)
    mixed = (gates[:, 0:1] * out_first + gates[:, 1:2] * out_second).astype(jnp.bfloat16)
    dot_terms = jnp.stack(
        [jnp.sum(grad_out * out_first, axis=1), jnp.sum(grad_out * out_second, axis=1)], axis=1
    )
    grad_gates = lax.psum(dot_terms, "cuts")
    grad_hidden = lax.dot_general(
        d_rows, down_w, (((1,), (1,)), ((), ())), preferred_element_type=jnp.float32
    )
    grad_gate_pre = (
        grad_hidden * up_pre * sigmoid_gate * (1.0 + gate_pre * (1.0 - sigmoid_gate))
    ).astype(jnp.bfloat16)
    grad_up_pre = (grad_hidden * activated).astype(jnp.bfloat16)
    grad_down = lax.dot_general(
        hidden, d_rows, (((0,), (0,)), ((), ())), preferred_element_type=jnp.float32
    ).astype(jnp.bfloat16)
    grad_gate_w = lax.dot_general(
        x_rows, grad_gate_pre, (((0,), (0,)), ((), ())), preferred_element_type=jnp.float32
    ).astype(jnp.bfloat16)
    grad_up_w = lax.dot_general(
        x_rows, grad_up_pre, (((0,), (0,)), ((), ())), preferred_element_type=jnp.float32
    ).astype(jnp.bfloat16)
    row_partial = lax.dot_general(
        grad_gate_pre, gate_w, (((1,), (1,)), ((), ())), preferred_element_type=jnp.float32
    )
    row_partial = row_partial + lax.dot_general(
        grad_up_pre, up_w, (((1,), (1,)), ((), ())), preferred_element_type=jnp.float32
    )
    grad_home = send_home(row_partial)
    grad_tokens = (
        gates[:, 0:1] * grad_home[destination[:, 0]].astype(jnp.float32)
        + gates[:, 1:2] * grad_home[destination[:, 1]].astype(jnp.float32)
    ).astype(jnp.bfloat16)
    return (mixed, grad_tokens, grad_gates, grad_gate_w[None], grad_up_w[None], grad_down[None])


def solution(mesh):
    return jax.shard_map(
        local,
        mesh=mesh,
        in_specs=(
            P("expert", "cuts"),
            P("expert", None),
            P("expert", None),
            P("expert", "cuts"),
            P("expert", None, "cuts"),
            P("expert", None, "cuts"),
            P("expert", "cuts", None),
        ),
        out_specs=(
            P("expert", "cuts"),
            P("expert", "cuts"),
            P("expert", None),
            P("expert", None, "cuts"),
            P("expert", None, "cuts"),
            P("expert", "cuts", None),
        ),
        check_vma=False,
    )
```

profile of v0, /device:TPU:0, one launch (start us, length us, event | category | flops | bytes accessed | tf_op | source)
XLA Modules:
  0.0 371.7 jit_solution(16859567116568932094)
XLA Ops:
  10.4 11.8 %all_to_all.48 = bf16[8,64,256]{2,1,0:T(8,128)(2,1)} all-to-all(bf16[8,64,256]{2,1,0:T(8,128)(2,1)S(1)} %bitcast.70), channel_id=1, replica_groups=mesh['expert'=8,'cuts'=16] {'expert'}, dimensions={0} | all-to-all | bytes 524288 | tf_op jit(solution)/shard_map/all_to_all | solution.py:37
  23.0 1.1 fusion.16
  24.2 1.1 fusion.13
  25.3 10.6 %all_to_all.49 = bf16[8,64,256]{2,1,0:T(8,128)(2,1)} all-to-all(bf16[8,64,256]{2,1,0:T(8,128)(2,1)S(1)} %bitcast.73), channel_id=1, replica_groups=mesh['expert'=8,'cuts'=16] {'expert'}, dimensions={0} | all-to-all | bytes 524288 | tf_op jit(solution)/shard_map/all_to_all | solution.py:38
  36.0 43.9 %all-gather.3.cloned.1.call-done = bf16[512,4096]{1,0:T(8,128)(2,1)} async-done(((bf16[512,256]{1,0:T(8,128)(2,1)}), bf16[512,4096]{1,0:T(8,128)(2,1)}) %all-gather.3.cloned.1.call-update) | async-done | bytes 4194320 | tf_op jit(solution)/shard_map/all_gather | solution.py:41
  79.9 5.9 %fusion.11 = f32[512,512]{1,0:T(8,128)S(1)} fusion(bf16[512,4096]{1,0:T(8,128)(2,1)} %all-gather.3.cloned.1.call-done, bf16[1,4096,512]{2,1,0:T(8,128)(2,1)} %param.11), kind=kOutput, calls=%fused_computation.20 | convolution fusion | flops 2147483648 | bytes 9437184 | tf_op jit(solution)/shard_map/dot_general | solution.py:54
  85.8 3.3 fusion.7
  89.1 49.1 %all-gather.5.cloned.1.call-done = bf16[512,4096]{1,0:T(8,128)(2,1)} async-done(((bf16[512,256]{1,0:T(8,128)(2,1)}), bf16[512,4096]{1,0:T(8,128)(2,1)}) %all-gather.5.cloned.1.call-update) | async-done | bytes 4194320 | tf_op jit(solution)/shard_map/all_gather | solution.py:42
  138.3 6.6 %multiply_convert_fusion = (bf16[512,512]{1,0:T(8,128)(2,1)S(1)}, bf16[512,512]{1,0:T(8,128)(2,1)S(1)}, bf16[512,512]{1,0:T(8,128)(2,1)S(1)}) fusion(f32[512,512]{1,0:T(8,128)S(1)} %fusion.11, f32[512,512]{1,0:T(8,128)} %fusion.7, bf16[512,4096]{1,0:T(8,128)(2,1)} %all-gather.5.cloned.1.call-done, bf16[1,512,4096]{2,1,0:T(8,128)(2,1)} %param.13), kind=kOutput, calls=%fused_computation.25 | convolution fusion | flops 2151415808 | bytes 12058624 | tf_op jit(solution)/shard_map/dot_general | solution.py:68
  144.9 2.4 fusion.9
  147.3 4.5 %add_convert_fusion = bf16[512,4096]{1,0:T(8,128)(2,1)} fusion(f32[512,4096]{1,0:T(8,128)S(1)} %fusion.9, bf16[512,512]{1,0:T(8,128)(2,1)S(1)} %get-tuple-element.8, bf16[1,4096,512]{2,1,0:T(8,128)(2,1)S(1)} %copy-done.3), kind=kOutput, calls=%fused_computation.4 | convolution fusion | flops 2151677952 | bytes 17301504 | tf_op jit(solution)/shard_map/dot_general | solution.py:87
  152.1 6.6 %convolution_convert_fusion.3 = bf16[512,4096]{1,0:T(8,128)(2,1)} fusion(bf16[512,512]{1,0:T(8,128)(2,1)S(1)} %get-tuple-element.10, bf16[1,512,4096]{2,1,0:T(8,128)(2,1)} %param.13), kind=kOutput, calls=%fused_computation.8 | convolution fusion | flops 2149580800 | bytes 8912896 | tf_op jit(solution)/shard_map/dot_general | solution.py:59
  158.7 6.7 %fusion.2 = bf16[1,512,4096]{2,1,0:T(8,128)(2,1)} fusion(bf16[512,512]{1,0:T(8,128)(2,1)S(1)} %get-tuple-element.10, bf16[512,4096]{1,0:T(8,128)(2,1)} %all-gather.5.cloned.1.call-done), kind=kOutput, calls=%fused_computation.11 | convolution fusion | flops 2149580800 | bytes 8912896 | tf_op jit(solution)/shard_map/dot_general | solution.py:75
  165.4 64.5 %reduce-scatter.5.cloned.1.call-done = bf16[512,256]{1,0:T(8,128)(2,1)} async-done(((bf16[512,4096]{1,0:T(8,128)(2,1)}), bf16[512,256]{1,0:T(8,128)(2,1)}) %reduce-scatter.5.cloned.1.call-update) | async-done | bytes 262160 | tf_op jit(solution)/shard_map/reduce_scatter | solution.py:46
  229.9 4.3 %all-to-all-start.3 = ((bf16[8,64,256]{2,1,0:T(8,128)(2,1)}), bf16[8,64,256]{2,1,0:T(8,128)(2,1)S(1)}, u32[]{:S(2)}, u32[]{:S(2)}) async-start(bf16[8,64,256]{2,1,0:T(8,128)(2,1)} %bitcast.75), calls=%async_computation.5 | async-start | bytes 524288 | tf_op jit(solution)/shard_map/all_to_all | solution.py:49
  234.2 6.6 %fusion = bf16[1,4096,512]{2,1,0:T(8,128)(2,1)} fusion(bf16[512,4096]{1,0:T(8,128)(2,1)} %all-gather.3.cloned.1.call-done, bf16[512,512]{1,0:T(8,128)(2,1)S(1)} %get-tuple-element.9), kind=kOutput, calls=%fused_computation.9 | convolution fusion | flops 2149580800 | bytes 8912896 | tf_op jit(solution)/shard_map/dot_general | solution.py:78
  240.8 70.6 %reduce-scatter.3.cloned.1.call-done = bf16[512,256]{1,0:T(8,128)(2,1)} async-done(((bf16[512,4096]{1,0:T(8,128)(2,1)}), bf16[512,256]{1,0:T(8,128)(2,1)}) %reduce-scatter.3.cloned.1.call-update) | async-done | bytes 262160 | tf_op jit(solution)/shard_map/reduce_scatter | solution.py:46
  311.4 4.3 %all-to-all-start.1 = ((bf16[8,64,256]{2,1,0:T(8,128)(2,1)}), bf16[8,64,256]{2,1,0:T(8,128)(2,1)S(1)}, u32[]{:S(2)}, u32[]{:S(2)}) async-start(bf16[8,64,256]{2,1,0:T(8,128)(2,1)} %bitcast.74), calls=%async_computation.2 | async-start | bytes 524288 | tf_op jit(solution)/shard_map/all_to_all | solution.py:49
  315.6 6.6 %fusion.1 = bf16[1,4096,512]{2,1,0:T(8,128)(2,1)} fusion(bf16[512,4096]{1,0:T(8,128)(2,1)} %all-gather.3.cloned.1.call-done, bf16[512,512]{1,0:T(8,128)(2,1)S(1)} %get-tuple-element.8), kind=kOutput, calls=%fused_computation.10 | convolution fusion | flops 2149580800 | bytes 8912896 | tf_op jit(solution)/shard_map/dot_general | solution.py:81
  322.3 0.8 gather_fusion.2
  323.1 0.8 gather_fusion.3
  324.0 0.8 gather_fusion.1
  324.8 0.8 gather_fusion
  326.5 38.7 %psum.7 = f32[128,2]{0,1:T(2,128)} all-reduce(f32[128,2]{0,1:T(2,128)S(1)} %pad_maximum_fusion), channel_id=1, replica_groups=mesh['expert'=8,'cuts'=16] {'cuts'}, use_global_device_ids=true, to_apply=%region_7.8 | all-reduce | flops 256 | bytes 2048 | tf_op jit(solution)/shard_map/psum | solution.py:67
  (40 shorter events, 5.2 us)
Async XLA Ops:
  7.2 3.0 copy-start
  7.2 72.7 %all-gather.3.cloned.1.call-start = ((), (), s32[]{:S(2)}) async-start(), calls=%async_computation.6 | async-start | bytes 4456448 | tf_op jit(solution)/shard_map/all_gather | solution.py:41
  22.2 116.0 %all-gather.5.cloned.1.call-start = ((), (), s32[]{:S(2)}) async-start(), calls=%async_computation.8 | async-start | bytes 4456448 | tf_op jit(solution)/shard_map/all_gather | solution.py:42
  35.9 194.0 %reduce-scatter.5.cloned.1.call-start = ((), (), s32[]{:S(2)}) async-start(), calls=%async_computation.9 | async-start | bytes 4456448 | tf_op jit(solution)/shard_map/reduce_scatter | solution.py:46
  79.9 5.9 %copy-start.2 = (bf16[1,4096,512]{2,1,0:T(8,128)(2,1)S(1)}, bf16[1,4096,512]{2,1,0:T(8,128)(2,1)}, u32[]{:S(2)}) copy-start(bf16[1,4096,512]{2,1,0:T(8,128)(2,1)} %param.12) | copy-start | bytes 12582916
  79.9 5.9 %copy-start.5 = (bf16[512,4096]{1,0:T(8,128)(2,1)S(1)}, bf16[512,4096]{1,0:T(8,128)(2,1)}, u32[]{:S(2)}) copy-start(bf16[512,4096]{1,0:T(8,128)(2,1)} %all-gather.3.cloned.1.call-done) | copy-start | bytes 12582916
  138.3 6.6 %copy-start.1 = (bf16[1,4096,512]{2,1,0:T(8,128)(2,1)S(1)}, bf16[1,4096,512]{2,1,0:T(8,128)(2,1)}, u32[]{:S(2)}) copy-start(bf16[1,4096,512]{2,1,0:T(8,128)(2,1)} %param.11) | copy-start | bytes 12582916
  144.8 2.4 copy-start.3
  151.8 159.5 %reduce-scatter.3.cloned.1.call-start = ((), (), s32[]{:S(2)}) async-start(), calls=%async_computation.7 | async-start | bytes 4456448 | tf_op jit(solution)/shard_map/reduce_scatter | solution.py:46
  229.9 81.5 %all-to-all-start.3 = ((bf16[8,64,256]{2,1,0:T(8,128)(2,1)}), bf16[8,64,256]{2,1,0:T(8,128)(2,1)S(1)}, u32[]{:S(2)}, u32[]{:S(2)}) async-start(bf16[8,64,256]{2,1,0:T(8,128)(2,1)} %bitcast.75), calls=%async_computation.5 | async-start | bytes 524288 | tf_op jit(solution)/shard_map/all_to_all | solution.py:49
  311.4 12.6 %all-to-all-start.1 = ((bf16[8,64,256]{2,1,0:T(8,128)(2,1)}), bf16[8,64,256]{2,1,0:T(8,128)(2,1)S(1)}, u32[]{:S(2)}, u32[]{:S(2)}) async-start(bf16[8,64,256]{2,1,0:T(8,128)(2,1)} %bitcast.74), calls=%async_computation.2 | async-start | bytes 524288 | tf_op jit(solution)/shard_map/all_to_all | solution.py:49
  315.6 10.0 %copy-start.4 = (bf16[128,256]{1,0:T(8,128)(2,1)S(1)}, bf16[128,256]{1,0:T(8,128)(2,1)}, u32[]{:S(2)}) copy-start(bf16[128,256]{1,0:T(8,128)(2,1)} %param.10) | copy-start | bytes 196612
Sparse Core Ops, SparseCore 0:
  22.4 57.4 all-gather.2
  82.0 56.2 all-gather.4
  152.0 77.9 reduce-scatter.4
  233.7 77.6 reduce-scatter.2
where the time goes:
time: 373 us; the launch traced here: 372 us
  waiting for transfers between devices  228 us (61%)
  blocking collectives  61.1 us (16%)
  matrix products  51.7 us (14%)
  between operations  13.9 us (4%)
  starting transfers between devices  8.85 us (2%)
  local copies, waits for them, and re-layouts  5.66 us (2%)
    reduce_scatter x2, waiting for transfers between devices, send_home(): lax.psum_scatter(partial_value.astype(jnp.bfloat16), 'cuts', scatter_dime...  135 us
    all_gather x1, waiting for transfers between devices, local(): lax.all_gather(d_recv, 'cuts', axis=1, tiled=True)  49.1 us
    all_gather x1, waiting for transfers between devices, local(): lax.all_gather(x_recv, 'cuts', axis=1, tiled=True)  43.9 us
    psum x1, blocking collectives, local(): grad_gates = lax.psum(dot_terms, 'cuts')  38.7 us
    all_to_all x1, blocking collectives, local(): lax.all_to_all(x_send, 'expert', split_axis=0, concat_axis=0, tiled=True)  11.8 us
    all_to_all x1, blocking collectives, local(): lax.all_to_all(d_send, 'expert', split_axis=0, concat_axis=0, tiled=True)  10.6 us
    all_to_all x2, starting transfers between devices, send_home(): lax.all_to_all(owned_sum, 'expert', split_axis=0, concat_axis=0, tiled=True)  8.51 us
  transfers between devices with their start and end apart: 6, of which 4 were waited for; matrix products, arithmetic and copies ran while one was open for 11% of the time, Pallas kernels for 0%

commit v1 on v0

v1 whole, which is shorter than its diff:
```python
import functools

import jax
import jax.numpy as jnp
from jax import lax
from jax.experimental import pallas as pl
from jax.experimental.pallas import tpu as pltpu
from jax.sharding import PartitionSpec as P

MESH = pl.DeviceIdType.MESH
BF = jnp.bfloat16
F32 = jnp.float32
N = 4
SLOT = 64
TB = 128
FW = 256
HID = 512
ORDER = ((0, 1, 2), (1, 2, 0), (2, 0, 1))
ROWS_X = ((0, 48), (48, 48), (96, 32))
ROWS_C = ((0, 48), (48, 32), (80, 48))


def dot(a, b):
    return jnp.dot(a, b, preferred_element_type=F32)


def dot_nt(a, b):
    return lax.dot_general(a, b, (((1,), (1,)), ((), ())), preferred_element_type=F32)


def dot_tn(a, b):
    return lax.dot_general(a, b, (((0,), (0,)), ((), ())), preferred_element_type=F32)


def layer_kernel(
    x_in, c_in, route_in, gates_in, wg_in, wu_in, wd_in,
    mixed_out, gtok_out, ggate_out, xr_out, dr_out, hid_out, ggp_out, gup_out,
    gx, gc, xr, dr, sx, sc, wg, wu, wd, fa, fb, fh, fg, hid, ggp, gup,
    lm0, lm1, lm2, lg0, lg1, lg2, meta, mine, pick, back, gslot, qy, qz, qe,
    send_sem, recv_sem, local_sem,
):
    ei, ci = lax.axis_index("expert"), lax.axis_index("cuts")
    own = (ei // 2, ci // N, ci % N)
    core = ei % 2
    partner = ei + 1 - 2 * core
    used = [0, 0]

    def at(axis, step):
        moved = (own[axis] + step) % N
        if axis == 0:
            return (moved * 2 + core, ci)
        if axis == 1:
            return (ei, moved * N + own[2])
        return (ei, own[1] * N + moved)

    def remote(src, dst, device):
        index = used[0]
        used[0] += 1
        copy = pltpu.make_async_remote_copy(
            src_ref=src, dst_ref=dst, send_sem=send_sem.at[index], recv_sem=recv_sem.at[index],
            device_id=device, device_id_type=MESH,
        )
        copy.start()
        return copy

    def nearby(src, dst):
        index = used[1]
        used[1] += 1
        copy = pltpu.make_async_copy(src, dst, local_sem.at[index])
        copy.start()
        return copy

    def region(rest, axis, place, half, rows):
        index = [own[0], own[1], own[2]]
        index[axis] = place
        for other in rest:
            index[other] = slice(None)
        lanes = slice(None)
        if half is not None:
            if rest:
                index[min(rest)] = pl.ds(2 * half, 2)
            else:
                lanes = pl.ds(half * (FW // 2), FW // 2)
        return (*index, pl.ds(*rows), lanes)

    def gather(buf, split):
        sent = []

        def begin(colour, stage):
            axis, rest = ORDER[colour][stage], ORDER[colour][:stage]
            made = []
            for step, half in ((1, 0), (-1, 1), (1, 1), (-1, 0)):
                part = buf.at[region(rest, axis, own[axis], half, split[colour])]
                made.append(remote(part, part, at(axis, step)))
            sent.extend(made)
            return made

        going = [begin(colour, 0) for colour in range(3)]
        yield
        for stage in range(3):
            passed = []
            for colour in range(3):
                axis, rest = ORDER[colour][stage], ORDER[colour][:stage]
                going[colour][0].wait_recv()
                part = buf.at[region(rest, axis, (own[axis] - 1) % N, 0, split[colour])]
                up = remote(part, part, at(axis, 1))
                going[colour][1].wait_recv()
                part = buf.at[region(rest, axis, (own[axis] + 1) % N, 1, split[colour])]
                down = remote(part, part, at(axis, -1))
                passed.append((up, down))
                sent.extend((up, down))
            yield
            for colour in range(3):
                going[colour][2].wait_recv()
                going[colour][3].wait_recv()
                passed[colour][0].wait_recv()
                passed[colour][1].wait_recv()
                if stage < 2:
                    going[colour] = begin(colour, stage + 1)
            yield
        for copy in sent:
            copy.wait_send()
        yield

    def scatter(buf, lands, split):
        sent = []

        def land(stage, slot, half, rows):
            if stage == 0:
                return lands[0].at[slot, pl.ds(2 * half, 2), :, pl.ds(*rows), :]
            if stage == 1:
                return lands[1].at[slot, pl.ds(2 * half, 2), pl.ds(*rows), :]
            return lands[2].at[slot, pl.ds(*rows), pl.ds(half * (FW // 2), FW // 2)]

        def begin(colour, stage):
            axis, rest, rows = ORDER[colour][2 - stage], ORDER[colour][: 2 - stage], split[colour]
            made = []
            for step, far, slot, half in ((1, 2, 0, 0), (-1, 2, 0, 1), (1, 1, 1, 1), (-1, -1, 2, 0)):
                part = buf.at[region(rest, axis, (own[axis] + far) % N, half, rows)]
                made.append(remote(part, land(stage, slot, half, rows), at(axis, step)))
            sent.extend(made)
            return made

        def pieces(colour, stage, place, first, count):
            axis, rest, rows = ORDER[colour][2 - stage], ORDER[colour][: 2 - stage], split[colour]
            outer = sorted(rest)

            def one(i):
                index = [own[0], own[1], own[2]]
                index[axis] = place
                if stage == 0:
                    index[outer[0]], index[outer[1]] = i // N, i % N
                    where = (i // N, i % N)
                elif stage == 1:
                    index[outer[0]] = i
                    where = (i,)
                else:
                    where = ()
                return (*index, pl.ds(*rows)), (*where, pl.ds(*rows))

            return one

        def add_half(colour, stage, place, half):
            one = pieces(colour, stage, place, 0, 0)
            if stage == 2:
                lanes = pl.ds(half * (FW // 2), FW // 2)
                here, there = one(0)
                total = buf[(*here, lanes)].astype(F32) + lands[2][(0, *there, lanes)].astype(F32)
                buf[(*here, lanes)] = total.astype(BF)
                return
            count = 8 if stage == 0 else 2

            def body(i, carry):
                here, there = one(i + half * count)
                total = buf[(*here, slice(None))].astype(F32) + lands[stage][(0, *there, slice(None))].astype(F32)
                buf[(*here, slice(None))] = total.astype(BF)
                return carry

            lax.fori_loop(0, count, body, 0)

        def add_own(colour, stage):
            axis = ORDER[colour][2 - stage]
            one = pieces(colour, stage, own[axis], 0, 0)

            def body(i, carry):
                here, there = one(i)
                total = (
                    buf[(*here, slice(None))].astype(F32)
                    + lands[stage][(1, *there, slice(None))].astype(F32)
                    + lands[stage][(2, *there, slice(None))].astype(F32)
                )
                buf[(*here, slice(None))] = total.astype(BF)
                return carry

            if stage == 2:
                body(0, 0)
            else:
                lax.fori_loop(0, 16 if stage == 0 else 4, body, 0)

        going = [begin(colour, 0) for colour in range(3)]
        yield
        for stage in range(3):
            passed = []
            for colour in range(3):
                axis, rest, rows = ORDER[colour][2 - stage], ORDER[colour][: 2 - stage], split[colour]
                going[colour][0].wait_recv()
                place = (own[axis] + 1) % N
                add_half(colour, stage, place, 0)
                up = remote(buf.at[region(rest, axis, place, 0, rows)], land(stage, 1, 0, rows), at(axis, 1))
                going[colour][1].wait_recv()
                place = (own[axis] - 1) % N
                add_half(colour, stage, place, 1)
                down = remote(buf.at[region(rest, axis, place, 1, rows)], land(stage, 2, 1, rows), at(axis, -1))
                passed.append((up, down))
                sent.extend((up, down))
            yield
            for colour in range(3):
                going[colour][2].wait_recv()
                going[colour][3].wait_recv()
                passed[colour][0].wait_recv()
                passed[colour][1].wait_recv()
                add_own(colour, stage)
                if stage < 2:
                    going[colour] = begin(colour, stage + 1)
            yield
        for copy in sent:
            copy.wait_send()
        yield

    load_x = nearby(x_in, gx.at[own])
    load_c = nearby(c_in, gc.at[own])
    load_wg = nearby(wg_in, wg)
    load_wu = nearby(wu_in, wu)
    load_wd = nearby(wd_in, wd)
    peers = [((ei + step) % 8, ci) for step in range(1, 8)]
    peers += [at(1, step) for step in (1, 2, 3)] + [at(2, step) for step in (1, 2, 3)]
    barrier = pltpu.get_barrier_semaphore()
    for device in peers:
        pl.semaphore_signal(barrier, inc=1, device_id=device, device_id_type=MESH)
    pl.semaphore_wait(barrier, len(peers))

    load_x.wait()
    tokens = gather(gx, ROWS_X)
    next(tokens)
    load_c.wait()
    cotangents = gather(gc, ROWS_C)
    next(cotangents)

    sub = lax.broadcasted_iota(jnp.int32, (TB, TB), 0)
    lane = lax.broadcasted_iota(jnp.int32, (TB, TB), 1)
    eye = sub == lane

    def to_row(column):
        return jnp.sum(jnp.where(eye, jnp.broadcast_to(column, (TB, TB)), 0.0), axis=0, keepdims=True)

    route = route_in[...].astype(F32)
    gates = gates_in[...]
    lane_f = lane.astype(F32)
    first = (route[:, 0:1] == lane_f).astype(F32)
    second = (route[:, 1:2] == lane_f).astype(F32)
    before = dot((lane < sub).astype(BF), (first + second).astype(BF))
    goal0 = route[:, 0:1] * SLOT + jnp.sum(first * before, axis=1, keepdims=True)
    goal1 = route[:, 1:2] * SLOT + jnp.sum(second * before, axis=1, keepdims=True)
    mine[...] = jnp.zeros((8, TB), F32)
    mine[0:1, :] = to_row(goal0)
    mine[1:2, :] = to_row(goal1)
    mine[2:3, :] = to_row(gates[:, 0:1])
    mine[3:4, :] = to_row(gates[:, 1:2])
    meta[ei] = mine[...]
    told = [remote(mine, meta.at[ei], ((ei + step) % 8, ci)) for step in range(1, 8)]

    next(tokens)
    next(cotangents)
    next(tokens)
    next(cotangents)
    next(tokens)
    next(cotangents)
    next(tokens)

    for copy in told:
        copy.wait()
    slot_f = jnp.where(sub < SLOT, ei * SLOT + sub, partner * SLOT + sub - SLOT).astype(F32)
    for x in range(N):
        block = 2 * x + core
        table = meta[block]
        chosen = ((table[0:1] == slot_f) | (table[1:2] == slot_f)).astype(F32)
        pick[x] = chosen.astype(BF)
        back[x] = chosen.T.astype(BF)
    own_f = (ei * SLOT + lax.broadcasted_iota(jnp.int32, (SLOT, TB), 0)).astype(F32)
    for group in range(8):
        block = 2 * (group % N) + (core if group < N else 1 - core)
        table = meta[block]
        weight = jnp.sum(
            jnp.where(table[0:1] == own_f, table[2:3], 0.0) + jnp.where(table[1:2] == own_f, table[3:4], 0.0),
            axis=1, keepdims=True,
        )
        gslot[pl.ds(group * SLOT, SLOT), :] = jnp.broadcast_to(weight, (SLOT, TB))

    next(tokens)
    next(cotangents)
    next(tokens)
    next(tokens)

    def compact(buf, stage_buf, rows, x):
        def body(i, carry):
            y, z = i // N, i % N
            got = dot(pick[x], buf[x, y, z]).astype(BF)
            rows[y, z, pl.ds(x * SLOT, SLOT), :] = got[:SLOT]
            stage_buf[x, y, z] = got[SLOT:]
            return carry

        lax.fori_loop(0, 16, body, 0, unroll=2)
        return remote(stage_buf.at[x], rows.at[:, :, pl.ds((N + x) * SLOT, SLOT), :], (partner, ci))

    swap_x = [compact(gx, sx, xr, x) for x in range(N)]
    next(cotangents)
    load_wg.wait()
    load_wu.wait()

    def products(half):
        rows = pl.ds(half * 256, 256)

        def body(y, carry):
            up = down = None
            for z in range(N):
                block = xr[y, z, rows, :]
                feature = pl.ds(pl.multiple_of((y * N + z) * FW, FW), FW)
                g, u = dot(block, wg[feature, :]), dot(block, wu[feature, :])
                up, down = (g, u) if up is None else (up + g, down + u)
            fa[rows, :] += up
            fb[rows, :] += down
            return carry

        fa[rows, :] = jnp.zeros((256, HID), F32)
        fb[rows, :] = jnp.zeros((256, HID), F32)
        lax.fori_loop(0, N, body, 0)

    products(0)
    for copy in swap_x:
        copy.wait()
    products(1)

    def activate(i, carry):
        rows = pl.ds(pl.multiple_of(i * 32, 32), 32)
        gate, up = fa[rows, :], fb[rows, :]
        s = jax.nn.sigmoid(gate)
        act = gate * s
        value = act * up
        fh[rows, :] = value
        hid[rows, :] = (value * gslot[rows, 0:1]).astype(BF)
        fa[rows, :] = up * s * (1.0 + gate * (1.0 - s))
        fb[rows, :] = act
        return carry

    lax.fori_loop(0, 16, activate, 0)
    load_wd.wait()

    def spread(buf, stage_buf, y, value):
        def body(z, carry):
            got = value(y, z).astype(BF)
            for x in range(N):
                buf[x, y, z, 0:SLOT, :] = got[x * SLOT:(x + 1) * SLOT]
                stage_buf[x, y, z] = got[(N + x) * SLOT:(N + x + 1) * SLOT]
            return carry

        lax.fori_loop(0, N, body, 0)
        return remote(stage_buf.at[:, y], buf.at[:, y, :, pl.ds(SLOT, SLOT), :], (partner, ci))

    def forward(y, z):
        return dot(hid[...], wd[:, pl.ds(pl.multiple_of((y * N + z) * FW, FW), FW)])

    swap_m = [spread(gx, sx, y, forward) for y in range(N)]

    next(cotangents)
    next(cotangents)
    swap_c = [compact(gc, sc, dr, x) for x in range(N)]

    def expand(buf, y):
        def body(i, carry):
            x, z = i // N, i % N
            buf[x, y, z] = dot(back[x], buf[x, y, z]).astype(BF)
            return carry

        lax.fori_loop(0, 16, body, 0, unroll=2)

    for y in range(N):
        swap_m[y].wait()
        expand(gx, y)
    combine_m = scatter(gx, (lm0, lm1, lm2), ROWS_X)
    next(combine_m)

    def hidden_grad(half):
        rows = pl.ds(half * 256, 256)

        def body(y, carry):
            total = None
            for z in range(N):
                feature = pl.ds(pl.multiple_of((y * N + z) * FW, FW), FW)
                g = dot_nt(dr[y, z, rows, :], wd[:, feature])
                total = g if total is None else total + g
            fg[rows, :] += total
            return carry

        fg[rows, :] = jnp.zeros((256, HID), F32)
        lax.fori_loop(0, N, body, 0)

    hidden_grad(0)
    for copy in swap_c:
        copy.wait()
    next(combine_m)
    hidden_grad(1)

    eye_q = eye

    def inner(j, carry):
        base = pl.multiple_of(j * TB, TB)
        terms = []
        for k in range(4):
            rows = pl.ds(pl.multiple_of(base + k * 32, 32), 32)
            plain = fg[rows, :]
            terms.append(jnp.sum(fh[rows, :] * plain, axis=1, keepdims=True))
            scaled = plain * gslot[rows, 0:1]
            ggp[rows, :] = (scaled * fa[rows, :]).astype(BF)
            gup[rows, :] = (scaled * fb[rows, :]).astype(BF)
        column = jnp.concatenate(terms, axis=0)
        row = jnp.sum(jnp.where(eye_q, jnp.broadcast_to(column, (TB, TB)), 0.0), axis=0, keepdims=True)
        qy[own[1], pl.ds(j, 1), :] = row
        return carry

    qy[own[1]] = jnp.zeros((8, TB), F32)
    for j in range(4):
        inner(j, 0)
    ask_y = [remote(qy.at[own[1]], qy.at[own[1]], at(1, step)) for step in (1, 2, 3)]
    next(combine_m)

    def rows_grad(y, z):
        feature = pl.ds(pl.multiple_of((y * N + z) * FW, FW), FW)
        total = dot_nt(ggp[...], wg[feature, :]) + dot_nt(gup[...], wu[feature, :])
        return total * gslot[:, 0:1]

    swap_g = [spread(gc, sc, y, rows_grad) for y in range(2)]
    next(combine_m)
    swap_g += [spread(gc, sc, y, rows_grad) for y in range(2, N)]
    save = [nearby(src, dst) for src, dst in ((xr, xr_out), (dr, dr_out), (hid, hid_out), (ggp, ggp_out), (gup, gup_out))]
    for y in range(N):
        swap_g[y].wait()
        expand(gc, y)
    combine_g = scatter(gc, (lg0, lg1, lg2), ROWS_C)
    next(combine_g)
    for copy in ask_y:
        copy.wait()
    qz[own[2]] = qy[0] + qy[1] + qy[2] + qy[3]
    ask_z = [remote(qz.at[own[2]], qz.at[own[2]], at(2, step)) for step in (1, 2, 3)]
    next(combine_m)
    next(combine_g)
    next(combine_m)
    next(combine_m)
    mixed_out[...] = gx[own]
    for copy in ask_z:
        copy.wait()
    qe[ei] = qz[0] + qz[1] + qz[2] + qz[3]
    ask_e = [remote(qe.at[ei], qe.at[ei], ((ei + step) % 8, ci)) for step in range(1, 8)]
    next(combine_g)
    next(combine_g)
    next(combine_g)
    for copy in ask_e:
        copy.wait()
    odd = own[0] % 2
    sums = [jnp.zeros((TB, TB), F32), jnp.zeros((TB, TB), F32)]
    slot_lane = lane - SLOT * odd
    inside = (slot_lane >= 0) & (slot_lane < SLOT)
    for e in range(8):
        line = own[0] // 2 + jnp.where(core == e % 2, 0, 2)
        row = qe[e, pl.ds(line, 1), :]
        target = (slot_lane + e * SLOT).astype(F32)
        for k, goal in enumerate((goal0, goal1)):
            sums[k] += jnp.where(inside & (goal == target), row, 0.0)
    ggate_out[:, 0:1] = jnp.sum(sums[0], axis=1, keepdims=True)
    ggate_out[:, 1:2] = jnp.sum(sums[1], axis=1, keepdims=True)
    next(combine_g)
    next(combine_g)
    next(combine_m)
    next(combine_g)
    gtok_out[...] = gc[own]
    for copy in save:
        copy.wait()


def weight_kernel(xr, dr, hid, ggp, gup, gw_out, uw_out, dw_out):
    block = xr[0, 0]
    gw_out[0] = dot_tn(block, ggp[...]).astype(BF)
    uw_out[0] = dot_tn(block, gup[...]).astype(BF)
    dw_out[0] = dot_tn(hid[...], dr[0, 0]).astype(BF)


def local(tokens, routing, gates, cotangent, w_gate, w_up, w_down):
    rows = 8 * SLOT
    features = N * N * FW
    vmem, anywhere = pl.BlockSpec(memory_space=pltpu.VMEM), pl.BlockSpec(memory_space=pl.ANY)
    grid_buf = pltpu.VMEM((N, N, N, TB, FW), BF)
    row_buf = pltpu.VMEM((N, N, rows, FW), BF)
    stage_buf = pltpu.VMEM((N, N, N, SLOT, FW), BF)
    f_buf = pltpu.VMEM((rows, HID), F32)
    h_buf = pltpu.VMEM((rows, HID), BF)
    lands = [pltpu.VMEM((3, N, N, TB, FW), BF), pltpu.VMEM((3, N, TB, FW), BF), pltpu.VMEM((3, TB, FW), BF)]
    struct = jax.ShapeDtypeStruct
    mixed, grad_tokens, grad_gates, xr, dr, hid, ggp, gup = pl.pallas_call(
        layer_kernel,
        out_shape=(
            struct((TB, FW), BF), struct((TB, FW), BF), struct((TB, 2), F32),
            struct((N, N, rows, FW), BF), struct((N, N, rows, FW), BF),
            struct((rows, HID), BF), struct((rows, HID), BF), struct((rows, HID), BF),
        ),
        in_specs=[anywhere, anywhere, vmem, vmem, anywhere, anywhere, anywhere],
        out_specs=(vmem, vmem, vmem, anywhere, anywhere, anywhere, anywhere, anywhere),
        scratch_shapes=[
            grid_buf, grid_buf, row_buf, row_buf, stage_buf, stage_buf,
            pltpu.VMEM((features, HID), BF), pltpu.VMEM((features, HID), BF), pltpu.VMEM((HID, features), BF),
            f_buf, f_buf, f_buf, f_buf, h_buf, h_buf, h_buf,
            *lands, *lands,
            pltpu.VMEM((8, 8, TB), F32), pltpu.VMEM((8, TB), F32),
            pltpu.VMEM((N, TB, TB), BF), pltpu.VMEM((N, TB, TB), BF), pltpu.VMEM((rows, TB), F32),
            pltpu.VMEM((N, 8, TB), F32), pltpu.VMEM((N, 8, TB), F32), pltpu.VMEM((8, 8, TB), F32),
            pltpu.SemaphoreType.DMA((256,)), pltpu.SemaphoreType.DMA((256,)), pltpu.SemaphoreType.DMA((16,)),
        ],
        compiler_params=pltpu.CompilerParams(collective_id=0, has_side_effects=True, vmem_limit_bytes=60 * 2**20),
        name="layer",
    )(tokens, cotangent, routing, gates, w_gate[0], w_up[0], w_down[0])
    whole = lambda c: (0, 0)
    piece = pl.BlockSpec((1, 1, rows, FW), lambda c: (c // N, c % N, 0, 0))
    small = pl.BlockSpec((rows, HID), whole)
    tall = pl.BlockSpec((1, FW, HID), lambda c: (0, c, 0))
    grad_gate_w, grad_up_w, grad_down = pl.pallas_call(
        weight_kernel,
        grid=(N * N,),
        out_shape=(struct((1, features, HID), BF), struct((1, features, HID), BF), struct((1, HID, features), BF)),
        in_specs=[piece, piece, small, small, small],
        out_specs=(tall, tall, pl.BlockSpec((1, HID, FW), lambda c: (0, 0, c))),
        name="weight_grads",
    )(xr, dr, hid, ggp, gup)
    return (mixed, grad_tokens, grad_gates, grad_gate_w, grad_up_w, grad_down)


def solution(mesh):
    return jax.shard_map(
        local,
        mesh=mesh,
        in_specs=(
            P("expert", "cuts"),
            P("expert", None),
            P("expert", None),
            P("expert", "cuts"),
            P("expert", None, "cuts"),
            P("expert", None, "cuts"),
            P("expert", "cuts", None),
        ),
        out_specs=(
            P("expert", "cuts"),
            P("expert", "cuts"),
            P("expert", None),
            P("expert", None, "cuts"),
            P("expert", None, "cuts"),
            P("expert", "cuts", None),
        ),
        check_vma=False,
    )
```

time: 373 us -> 164 us (0.44)
  waiting for transfers between devices: 228 us -> 0 us
  Pallas kernels: 0 us -> 157 us
  blocking collectives: 61.1 us -> 0 us
  matrix products: 51.7 us -> 0 us
  between operations: 13.9 us -> 0.64 us
  starting transfers between devices: 8.85 us -> 0 us
    pallas_call x0 -> x2, Pallas kernels: none -> 157 us  [the longest x1 141 us: local(): pl.pallas_call(layer_kernel, out_shape=(struct((TB, FW), BF), struct((TB,...]
    reduce_scatter x2 -> x0, waiting for transfers between devices: 135 us -> none  [send_home(): lax.psum_scatter(partial_value.astype(jnp.bfloat16), 'cuts', scatter_dime...]
    all_gather x2 -> x0, waiting for transfers between devices: 93 us -> none  [the longest x1 49.1 us: local(): lax.all_gather(d_recv, 'cuts', axis=1, tiled=True)]
    dot_general x12 -> x0, matrix products: 51.7 us -> none  [the longest x1 6.72 us: local(): lax.dot_general(hidden, d_rows, (((0,), (0,)), ((), ())), preferred_eleme...]
    psum x1 -> x0, blocking collectives: 38.7 us -> none  [local(): grad_gates = lax.psum(dot_terms, 'cuts')]
    all_to_all x2 -> x0, blocking collectives: 22.4 us -> none  [the longest x1 11.8 us: local(): lax.all_to_all(x_send, 'expert', split_axis=0, concat_axis=0, tiled=True)]
    all_to_all x2 -> x0, starting transfers between devices: 8.51 us -> none  [send_home(): lax.all_to_all(owned_sum, 'expert', split_axis=0, concat_axis=0, tiled=True)]
    unnamed x13 -> x9, local copies, waits for them, and re-layouts: 0.82 us -> 5.57 us
  transfers between devices with their start and end apart: 6 -> 0, of which waited for: 4 -> 0; matrix products, arithmetic and copies ran while one was open for 11% -> 0% of each run, Pallas kernels for 0% -> 0%
where the time goes in v1:
time: 164 us
  Pallas kernels  157 us (96%)
  local copies, waits for them, and re-layouts  5.57 us (3%)
    pallas_call x1, Pallas kernels, local(): pl.pallas_call(layer_kernel, out_shape=(struct((TB, FW), BF), struct((TB,...  141 us
    pallas_call x1, Pallas kernels, local(): pl.pallas_call(weight_kernel, grid=(N * N,), out_shape=(struct((1, featur...  16 us
    unnamed x9, local copies, waits for them, and re-layouts  5.57 us

profile of v1, /device:TPU:0, one launch (start us, length us, event | category | flops | bytes accessed | tf_op | source)
XLA Modules:
  0.0 163.5 jit_solution(9292402855869125579)
XLA Ops:
  0.6 1.4 copy.13.route_in
  2.0 1.4 copy.14.gates_in
  3.5 141.3 %layer.1 = (bf16[128,256]{1,0:T(8,128)(2,1)}, bf16[128,256]{1,0:T(8,128)(2,1)}, f32[128,2]{1,0:T(8,128)}, bf16[4,4,512,256]{3,2,1,0:T(8,128)(2,1)}, bf16[4,4,512...) custom-call(bf16[128,256]{1,0:T(8,128)(2,1)} %x_in.1, ...), custom_call_target="tpu_custom_call" | custom-call | tf_op jit(solution)/shard_map/layer/pallas_call | solution.py:507
  144.8 1.5 copy.15
  146.3 0.0 copy-start.1
  146.3 0.0 copy-start
  146.3 16.0 %weight_grads.1 = (bf16[1,4096,512]{2,1,0:T(8,128)(2,1)}, bf16[1,4096,512]{2,1,0:T(8,128)(2,1)}, bf16[1,512,4096]{2,1,0:T(8,128)(2,1)}) custom-call(bf16[4,4,512,256]{3,2,1,0:T(8,128)(2,1)} %get-tuple-element.20.xr, bf16[4,4,512,256]{3,2,1,0:T(8,128)(2,1)} %get-tuple-element.21.dr, bf16[512,512]{1,0:T(8,128)(2,1)} %get-tuple-element.22.hid, ...), custom_call_target="tpu_custom_call" | custom-call | tf_op jit(solution)/shard_map/weight_grads/pallas_call | solution.py:533
  162.3 0.0 copy-done.1
  162.3 0.6 copy.18
  162.9 0.0 copy-done
  162.9 0.6 copy.19
Async XLA Ops:
  146.3 16.0 %copy-start.1 = (bf16[128,256]{1,0:T(8,128)(2,1)S(1)}, bf16[128,256]{1,0:T(8,128)(2,1)}, u32[]{:S(2)}) copy-start(bf16[128,256]{1,0:T(8,128)(2,1)} %get-tuple-element.40) | copy-start | bytes 196612
  146.3 16.6 %copy-start = (bf16[128,256]{1,0:T(8,128)(2,1)S(1)}, bf16[128,256]{1,0:T(8,128)(2,1)}, u32[]{:S(2)}) copy-start(bf16[128,256]{1,0:T(8,128)(2,1)} %get-tuple-element.41) | copy-start | bytes 196612

commit v2 on v1

--- a/solution.py
+++ b/solution.py
@@ -253,19 +253,22 @@
     def to_row(column):
         return jnp.sum(jnp.where(eye, jnp.broadcast_to(column, (TB, TB)), 0.0), axis=0, keepdims=True)
 
+    def to_column(row):
+        return jnp.sum(jnp.where(eye, jnp.broadcast_to(row, (TB, TB)), 0.0), axis=1, keepdims=True)
+
     route = route_in[...].astype(F32)
     gates = gates_in[...]
-    lane_f = lane.astype(F32)
-    first = (route[:, 0:1] == lane_f).astype(F32)
-    second = (route[:, 1:2] == lane_f).astype(F32)
-    before = dot((lane < sub).astype(BF), (first + second).astype(BF))
-    goal0 = route[:, 0:1] * SLOT + jnp.sum(first * before, axis=1, keepdims=True)
-    goal1 = route[:, 1:2] * SLOT + jnp.sum(second * before, axis=1, keepdims=True)
+    number = lax.broadcasted_iota(jnp.int32, (16, TB), 0).astype(F32)
+    first = (route[0:1] == number).astype(F32)
+    second = (route[1:2] == number).astype(F32)
+    before = dot((first + second).astype(BF), (sub < lane).astype(BF))
+    goal0 = route[0:1] * SLOT + jnp.sum(first * before, axis=0, keepdims=True)
+    goal1 = route[1:2] * SLOT + jnp.sum(second * before, axis=0, keepdims=True)
     mine[...] = jnp.zeros((8, TB), F32)
-    mine[0:1, :] = to_row(goal0)
-    mine[1:2, :] = to_row(goal1)
-    mine[2:3, :] = to_row(gates[:, 0:1])
-    mine[3:4, :] = to_row(gates[:, 1:2])
+    mine[0:1, :] = goal0
+    mine[1:2, :] = goal1
+    mine[2:3, :] = gates[0:1]
+    mine[3:4, :] = gates[1:2]
     meta[ei] = mine[...]
     told = [remote(mine, meta.at[ei], ((ei + step) % 8, ci)) for step in range(1, 8)]
 
@@ -302,14 +305,14 @@
     next(tokens)
 
     def compact(buf, stage_buf, rows, x):
-        def body(i, carry):
-            y, z = i // N, i % N
-            got = dot(pick[x], buf[x, y, z]).astype(BF)
-            rows[y, z, pl.ds(x * SLOT, SLOT), :] = got[:SLOT]
-            stage_buf[x, y, z] = got[SLOT:]
+        def body(y, carry):
+            got = [dot(pick[x], buf[x, y, z]).astype(BF) for z in range(N)]
+            for z in range(N):
+                rows[y, z, pl.ds(x * SLOT, SLOT), :] = got[z][:SLOT]
+                stage_buf[x, y, z] = got[z][SLOT:]
             return carry
 
-        lax.fori_loop(0, 16, body, 0, unroll=2)
+        lax.fori_loop(0, N, body, 0)
         return remote(stage_buf.at[x], rows.at[:, :, pl.ds((N + x) * SLOT, SLOT), :], (partner, ci))
 
     swap_x = [compact(gx, sx, xr, x) for x in range(N)]
@@ -317,28 +320,22 @@
     load_wg.wait()
     load_wu.wait()
 
-    def products(half):
-        rows = pl.ds(half * 256, 256)
-
-        def body(y, carry):
-            up = down = None
-            for z in range(N):
-                block = xr[y, z, rows, :]
-                feature = pl.ds(pl.multiple_of((y * N + z) * FW, FW), FW)
-                g, u = dot(block, wg[feature, :]), dot(block, wu[feature, :])
-                up, down = (g, u) if up is None else (up + g, down + u)
-            fa[rows, :] += up
-            fb[rows, :] += down
-            return carry
-
-        fa[rows, :] = jnp.zeros((256, HID), F32)
-        fb[rows, :] = jnp.zeros((256, HID), F32)
-        lax.fori_loop(0, N, body, 0)
-
-    products(0)
     for copy in swap_x:
         copy.wait()
-    products(1)
+
+    def products(y, carry):
+        up = down = None
+        for z in range(N):
+            feature = pl.ds(pl.multiple_of((y * N + z) * FW, FW), FW)
+            g, u = dot(xr[y, z], wg[feature, :]), dot(xr[y, z], wu[feature, :])
+            up, down = (g, u) if up is None else (up + g, down + u)
+        fa[...] += up
+        fb[...] += down
+        return carry
+
+    fa[...] = jnp.zeros((8 * SLOT, HID), F32)
+    fb[...] = jnp.zeros((8 * SLOT, HID), F32)
+    lax.fori_loop(0, N, products, 0)
 
     def activate(i, carry):
         rows = pl.ds(pl.multiple_of(i * 32, 32), 32)
@@ -376,12 +373,13 @@
     swap_c = [compact(gc, sc, dr, x) for x in range(N)]
 
     def expand(buf, y):
-        def body(i, carry):
-            x, z = i // N, i % N
-            buf[x, y, z] = dot(back[x], buf[x, y, z]).astype(BF)
+        def body(x, carry):
+            got = [dot(back[x], buf[x, y, z]).astype(BF) for z in range(N)]
+            for z in range(N):
+                buf[x, y, z] = got[z]
             return carry
 
-        lax.fori_loop(0, 16, body, 0, unroll=2)
+        lax.fori_loop(0, N, body, 0)
 
     for y in range(N):
         swap_m[y].wait()
@@ -389,28 +387,21 @@
     combine_m = scatter(gx, (lm0, lm1, lm2), ROWS_X)
     next(combine_m)
 
-    def hidden_grad(half):
-        rows = pl.ds(half * 256, 256)
-
-        def body(y, carry):
-            total = None
-            for z in range(N):
-                feature = pl.ds(pl.multiple_of((y * N + z) * FW, FW), FW)
-                g = dot_nt(dr[y, z, rows, :], wd[:, feature])
-                total = g if total is None else total + g
-            fg[rows, :] += total
-            return carry
-
-        fg[rows, :] = jnp.zeros((256, HID), F32)
-        lax.fori_loop(0, N, body, 0)
-
-    hidden_grad(0)
+    def hidden_grad(y, carry):
+        total = None
+        for z in range(N):
+            feature = pl.ds(pl.multiple_of((y * N + z) * FW, FW), FW)
+            g = dot_nt(dr[y, z], wd[:, feature])
+            total = g if total is None else total + g
+        fg[...] += total
+        return carry
+
     for copy in swap_c:
         copy.wait()
-    next(combine_m)
-    hidden_grad(1)
-
-    eye_q = eye
+    fg[...] = jnp.zeros((8 * SLOT, HID), F32)
+    lax.fori_loop(0, N // 2, hidden_grad, 0)
+    next(combine_m)
+    lax.fori_loop(N // 2, N, hidden_grad, 0)
 
     def inner(j, carry):
         base = pl.multiple_of(j * TB, TB)
@@ -423,7 +414,7 @@
             ggp[rows, :] = (scaled * fa[rows, :]).astype(BF)
             gup[rows, :] = (scaled * fb[rows, :]).astype(BF)
         column = jnp.concatenate(terms, axis=0)
-        row = jnp.sum(jnp.where(eye_q, jnp.broadcast_to(column, (TB, TB)), 0.0), axis=0, keepdims=True)
+        row = to_row(column)
         qy[own[1], pl.ds(j, 1), :] = row
         return carry
 
@@ -466,6 +457,7 @@
     for copy in ask_e:
         copy.wait()
     odd = own[0] % 2
+    goals = (to_column(goal0), to_column(goal1))
     sums = [jnp.zeros((TB, TB), F32), jnp.zeros((TB, TB), F32)]
     slot_lane = lane - SLOT * odd
     inside = (slot_lane >= 0) & (slot_lane < SLOT)
@@ -473,10 +465,10 @@
         line = own[0] // 2 + jnp.where(core == e % 2, 0, 2)
         row = qe[e, pl.ds(line, 1), :]
         target = (slot_lane + e * SLOT).astype(F32)
-        for k, goal in enumerate((goal0, goal1)):
+        for k, goal in enumerate(goals):
             sums[k] += jnp.where(inside & (goal == target), row, 0.0)
-    ggate_out[:, 0:1] = jnp.sum(sums[0], axis=1, keepdims=True)
-    ggate_out[:, 1:2] = jnp.sum(sums[1], axis=1, keepdims=True)
+    ggate_out[0:1] = to_row(jnp.sum(sums[0], axis=1, keepdims=True))
+    ggate_out[1:2] = to_row(jnp.sum(sums[1], axis=1, keepdims=True))
     next(combine_g)
     next(combine_g)
     next(combine_m)
@@ -486,11 +478,24 @@
         copy.wait()
 
 
-def weight_kernel(xr, dr, hid, ggp, gup, gw_out, uw_out, dw_out):
-    block = xr[0, 0]
-    gw_out[0] = dot_tn(block, ggp[...]).astype(BF)
-    uw_out[0] = dot_tn(block, gup[...]).astype(BF)
-    dw_out[0] = dot_tn(hid[...], dr[0, 0]).astype(BF)
+def weight_kernel(
+    xr, dr, hid, ggp, gup, mixed, gtok, ggate,
+    gw_out, uw_out, dw_out, mixed_out, gtok_out, ggate_out,
+    both, turned,
+):
+    @pl.when(pl.program_id(0) == 0)
+    def _():
+        both[:, :HID] = ggp[...]
+        both[:, HID:] = gup[...]
+        turned[...] = hid[...].T
+        mixed_out[...] = mixed[...]
+        gtok_out[...] = gtok[...]
+        ggate_out[...] = ggate[...]
+
+    grads = dot_tn(xr[0, 0], both[...])
+    gw_out[0] = grads[:, :HID].astype(BF)
+    uw_out[0] = grads[:, HID:].astype(BF)
+    dw_out[0] = dot(turned[...], dr[0, 0]).astype(BF)
 
 
 def local(tokens, routing, gates, cotangent, w_gate, w_up, w_down):
@@ -507,7 +512,7 @@
     mixed, grad_tokens, grad_gates, xr, dr, hid, ggp, gup = pl.pallas_call(
         layer_kernel,
         out_shape=(
-            struct((TB, FW), BF), struct((TB, FW), BF), struct((TB, 2), F32),
+            struct((TB, FW), BF), struct((TB, FW), BF), struct((2, TB), F32),
             struct((N, N, rows, FW), BF), struct((N, N, rows, FW), BF),
             struct((rows, HID), BF), struct((rows, HID), BF), struct((rows, HID), BF),
         ),
@@ -525,20 +530,26 @@
         ],
         compiler_params=pltpu.CompilerParams(collective_id=0, has_side_effects=True, vmem_limit_bytes=60 * 2**20),
         name="layer",
-    )(tokens, cotangent, routing, gates, w_gate[0], w_up[0], w_down[0])
+    )(tokens, cotangent, routing.T, gates.T, w_gate[0], w_up[0], w_down[0])
     whole = lambda c: (0, 0)
     piece = pl.BlockSpec((1, 1, rows, FW), lambda c: (c // N, c % N, 0, 0))
     small = pl.BlockSpec((rows, HID), whole)
     tall = pl.BlockSpec((1, FW, HID), lambda c: (0, c, 0))
-    grad_gate_w, grad_up_w, grad_down = pl.pallas_call(
+    owned = pl.BlockSpec((TB, FW), whole)
+    pair = pl.BlockSpec((2, TB), whole)
+    grad_gate_w, grad_up_w, grad_down, mixed, grad_tokens, grad_gates = pl.pallas_call(
         weight_kernel,
         grid=(N * N,),
-        out_shape=(struct((1, features, HID), BF), struct((1, features, HID), BF), struct((1, HID, features), BF)),
-        in_specs=[piece, piece, small, small, small],
-        out_specs=(tall, tall, pl.BlockSpec((1, HID, FW), lambda c: (0, 0, c))),
+        out_shape=(
+            struct((1, features, HID), BF), struct((1, features, HID), BF), struct((1, HID, features), BF),
+            struct((TB, FW), BF), struct((TB, FW), BF), struct((2, TB), F32),
+        ),
+        in_specs=[piece, piece, small, small, small, owned, owned, pair],
+        out_specs=(tall, tall, pl.BlockSpec((1, HID, FW), lambda c: (0, 0, c)), owned, owned, pair),
+        scratch_shapes=[pltpu.VMEM((rows, 2 * HID), BF), pltpu.VMEM((HID, rows), BF)],
         name="weight_grads",
-    )(xr, dr, hid, ggp, gup)
-    return (mixed, grad_tokens, grad_gates, grad_gate_w, grad_up_w, grad_down)
+    )(xr, dr, hid, ggp, gup, mixed, grad_tokens, grad_gates)
+    return (mixed, grad_tokens, grad_gates.T, grad_gate_w, grad_up_w, grad_down)
 
 
 def solution(mesh):

time: 164 us -> 143 us (0.87)
  Pallas kernels: 157 us -> 142 us
  local copies, waits for them, and re-layouts: 5.57 us -> 0 us
    pallas_call x1, Pallas kernels: 141 us -> 125 us  [local(): pl.pallas_call(layer_kernel, out_shape=(struct((TB, FW), BF), struct((TB,...]
    unnamed x9 -> x0, local copies, waits for them, and re-layouts: 5.57 us -> none
where the time goes in v2:
time: 143 us; the launch traced here: 142 us
  Pallas kernels  142 us (99%)
    pallas_call x1, Pallas kernels, local(): pl.pallas_call(layer_kernel, out_shape=(struct((TB, FW), BF), struct((TB,...  125 us
    pallas_call x1, Pallas kernels, local(): pl.pallas_call(weight_kernel, grid=(N * N,), out_shape=(struct((1, featur...  16.2 us

profile of v2, /device:TPU:0, one launch (start us, length us, event | category | flops | bytes accessed | tf_op | source)
XLA Modules:
  0.0 142.2 jit_solution(12543318539659230363)
XLA Ops:
  0.6 125.4 %layer.1 = (bf16[128,256]{1,0:T(8,128)(2,1)}, bf16[128,256]{1,0:T(8,128)(2,1)}, f32[2,128]{1,0:T(2,128)}, bf16[4,4,512,256]{3,2,1,0:T(8,128)(2,1)}, bf16[4,4,512...) custom-call(bf16[128,256]{1,0:T(8,128)(2,1)} %x_in.1, ...), custom_call_target="tpu_custom_call" | custom-call | tf_op jit(solution)/shard_map/layer/pallas_call | solution.py:512
  126.0 16.2 %weight_grads.1 = (bf16[1,4096,512]{2,1,0:T(8,128)(2,1)}, bf16[1,4096,512]{2,1,0:T(8,128)(2,1)}, bf16[1,512,4096]{2,1,0:T(8,128)(2,1)}, bf16[128,256]{1,0:T(8,12...) custom-call(bf16[4,4,512,256]{3,2,1,0:T(8,128)(2,1)} %get-tuple-element.20.xr, ...), custom_call_target="tpu_custom_call" | custom-call | tf_op jit(solution)/shard_map/weight_grads/pallas_call | solution.py:540

commit v3 on v2

--- a/solution.py
+++ b/solution.py
@@ -305,14 +305,12 @@
     next(tokens)
 
     def compact(buf, stage_buf, rows, x):
-        def body(y, carry):
-            got = [dot(pick[x], buf[x, y, z]).astype(BF) for z in range(N)]
+        chooser = pick[x]
+        for y in range(N):
             for z in range(N):
-                rows[y, z, pl.ds(x * SLOT, SLOT), :] = got[z][:SLOT]
-                stage_buf[x, y, z] = got[z][SLOT:]
-            return carry
-
-        lax.fori_loop(0, N, body, 0)
+                got = dot(chooser, buf[x, y, z]).astype(BF)
+                rows[y, z, x * SLOT:(x + 1) * SLOT, :] = got[:SLOT]
+                stage_buf[x, y, z] = got[SLOT:]
         return remote(stage_buf.at[x], rows.at[:, :, pl.ds((N + x) * SLOT, SLOT), :], (partner, ci))
 
     swap_x = [compact(gx, sx, xr, x) for x in range(N)]
@@ -373,13 +371,10 @@
     swap_c = [compact(gc, sc, dr, x) for x in range(N)]
 
     def expand(buf, y):
-        def body(x, carry):
-            got = [dot(back[x], buf[x, y, z]).astype(BF) for z in range(N)]
+        for x in range(N):
+            spreader = back[x]
             for z in range(N):
-                buf[x, y, z] = got[z]
-            return carry
-
-        lax.fori_loop(0, N, body, 0)
+                buf[x, y, z] = dot(spreader, buf[x, y, z]).astype(BF)
 
     for y in range(N):
         swap_m[y].wait()
@@ -399,9 +394,7 @@
     for copy in swap_c:
         copy.wait()
     fg[...] = jnp.zeros((8 * SLOT, HID), F32)
-    lax.fori_loop(0, N // 2, hidden_grad, 0)
-    next(combine_m)
-    lax.fori_loop(N // 2, N, hidden_grad, 0)
+    lax.fori_loop(0, N, hidden_grad, 0)
 
     def inner(j, carry):
         base = pl.multiple_of(j * TB, TB)
@@ -429,15 +422,15 @@
         total = dot_nt(ggp[...], wg[feature, :]) + dot_nt(gup[...], wu[feature, :])
         return total * gslot[:, 0:1]
 
-    swap_g = [spread(gc, sc, y, rows_grad) for y in range(2)]
-    next(combine_m)
-    swap_g += [spread(gc, sc, y, rows_grad) for y in range(2, N)]
+    swap_g = [spread(gc, sc, y, rows_grad) for y in range(N)]
     save = [nearby(src, dst) for src, dst in ((xr, xr_out), (dr, dr_out), (hid, hid_out), (ggp, ggp_out), (gup, gup_out))]
+    next(combine_m)
     for y in range(N):
         swap_g[y].wait()
         expand(gc, y)
     combine_g = scatter(gc, (lg0, lg1, lg2), ROWS_C)
     next(combine_g)
+    next(combine_m)
     for copy in ask_y:
         copy.wait()
     qz[own[2]] = qy[0] + qy[1] + qy[2] + qy[3]
@@ -492,10 +485,12 @@
         gtok_out[...] = gtok[...]
         ggate_out[...] = ggate[...]
 
-    grads = dot_tn(xr[0, 0], both[...])
-    gw_out[0] = grads[:, :HID].astype(BF)
-    uw_out[0] = grads[:, HID:].astype(BF)
-    dw_out[0] = dot(turned[...], dr[0, 0]).astype(BF)
+    for z in range(N):
+        part = slice(z * FW, (z + 1) * FW)
+        grads = dot_tn(xr[0, z], both[...])
+        gw_out[0, part] = grads[:, :HID].astype(BF)
+        uw_out[0, part] = grads[:, HID:].astype(BF)
+        dw_out[0, :, part] = dot(turned[...], dr[0, z]).astype(BF)
 
 
 def local(tokens, routing, gates, cotangent, w_gate, w_up, w_down):
@@ -532,20 +527,20 @@
         name="layer",
     )(tokens, cotangent, routing.T, gates.T, w_gate[0], w_up[0], w_down[0])
     whole = lambda c: (0, 0)
-    piece = pl.BlockSpec((1, 1, rows, FW), lambda c: (c // N, c % N, 0, 0))
+    piece = pl.BlockSpec((1, N, rows, FW), lambda c: (c, 0, 0, 0))
     small = pl.BlockSpec((rows, HID), whole)
-    tall = pl.BlockSpec((1, FW, HID), lambda c: (0, c, 0))
+    tall = pl.BlockSpec((1, N * FW, HID), lambda c: (0, c, 0))
     owned = pl.BlockSpec((TB, FW), whole)
     pair = pl.BlockSpec((2, TB), whole)
     grad_gate_w, grad_up_w, grad_down, mixed, grad_tokens, grad_gates = pl.pallas_call(
         weight_kernel,
-        grid=(N * N,),
+        grid=(N,),
         out_shape=(
             struct((1, features, HID), BF), struct((1, features, HID), BF), struct((1, HID, features), BF),
             struct((TB, FW), BF), struct((TB, FW), BF), struct((2, TB), F32),
         ),
         in_specs=[piece, piece, small, small, small, owned, owned, pair],
-        out_specs=(tall, tall, pl.BlockSpec((1, HID, FW), lambda c: (0, 0, c)), owned, owned, pair),
+        out_specs=(tall, tall, pl.BlockSpec((1, HID, N * FW), lambda c: (0, 0, c)), owned, owned, pair),
         scratch_shapes=[pltpu.VMEM((rows, 2 * HID), BF), pltpu.VMEM((HID, rows), BF)],
         name="weight_grads",
     )(xr, dr, hid, ggp, gup, mixed, grad_tokens, grad_gates)

time: 143 us -> 128 us (0.90)
  Pallas kernels: 142 us -> 127 us
    pallas_call x1, Pallas kernels: 125 us -> 115 us  [local(): pl.pallas_call(layer_kernel, out_shape=(struct((TB, FW), BF), struct((TB,...]
    pallas_call x1, Pallas kernels: 16.2 us -> 12 us  [local(): pl.pallas_call(weight_kernel, grid=(N,), out_shape=(struct((1, features,...]
where the time goes in v3:
time: 128 us
  Pallas kernels  127 us (99%)
    pallas_call x1, Pallas kernels, local(): pl.pallas_call(layer_kernel, out_shape=(struct((TB, FW), BF), struct((TB,...  115 us
    pallas_call x1, Pallas kernels, local(): pl.pallas_call(weight_kernel, grid=(N,), out_shape=(struct((1, features,...  12 us

profile of v3, /device:TPU:0, one launch (start us, length us, event | category | flops | bytes accessed | tf_op | source)
XLA Modules:
  0.0 127.8 jit_solution(16970183493391589103)
XLA Ops:
  0.6 115.2 %layer.1 = (bf16[128,256]{1,0:T(8,128)(2,1)}, bf16[128,256]{1,0:T(8,128)(2,1)}, f32[2,128]{1,0:T(2,128)}, bf16[4,4,512,256]{3,2,1,0:T(8,128)(2,1)}, bf16[4,4,512...) custom-call(bf16[128,256]{1,0:T(8,128)(2,1)} %x_in.1, ...), custom_call_target="tpu_custom_call" | custom-call | tf_op jit(solution)/shard_map/layer/pallas_call | solution.py:507
  115.8 12.0 %weight_grads.1 = (bf16[1,4096,512]{2,1,0:T(8,128)(2,1)}, bf16[1,4096,512]{2,1,0:T(8,128)(2,1)}, bf16[1,512,4096]{2,1,0:T(8,128)(2,1)}, bf16[128,256]{1,0:T(8,12...) custom-call(bf16[4,4,512,256]{3,2,1,0:T(8,128)(2,1)} %get-tuple-element.20.xr, ...), custom_call_target="tpu_custom_call" | custom-call | tf_op jit(solution)/shard_map/weight_grads/pallas_call | solution.py:535
